TPU v7x, 128 devices: a whole 4x4x4 slice. The times are simulated.
128 devices in a mesh: row: 8 (over z, core), col: 16 (over y, x).
Axes of the slice: x: 4, y: 4, z: 4, core: 2. Of those that a mesh axis runs over, the one named last changes fastest.
Arguments:
- snapshots: bfloat16 [4096, 32768], P('row', 'col'), may hold values from -14 to 14
- neighbours: int32 [4096, 128], P('row'), may hold values from 0 to 4095, all different within a row
- start_basis: float32 [32, 4096], replicated, may hold values from -6 to 6
Outputs:
- basis: float32 [32, 4096], P(None, 'row')
- rayleigh: float32 [32, 32], replicated
Inputs may be any that keep to these rules, and one draw needn't show every extreme that they name: `neighbours`: each row names 128 different snapshots.
All inputs are finite; a program needn't handle non-finite values.
Results may differ from a plain program's by a relative error of at most 0.00145.
Values may be sent and summed in bfloat16 or wider, within the bound.
No kernel may reach another device: no remote copies, remote signals or barrier semaphores. Data moves between devices by JAX's collectives and lax.ppermute only.
A program may use at most 128 MiB of HBM per device.

v0:
```python
import math
import jax
import jax.numpy as jnp
from jax import lax
from jax.sharding import PartitionSpec as P

FEATURES = 32768
LAGS = 64
ITERS = 2


def global_sum(value):
    return lax.psum(value, ("row", "col"))


def collect(columns):
    return lax.all_gather(columns, ("row", "col"), axis=1, tiled=True)


def shards(snapshots, neighbours, start_basis):
    row_count = lax.axis_size("row")
    col_count = lax.axis_size("col")
    row_at = lax.axis_index("row")
    col_at = lax.axis_index("col")
    lag_count = LAGS
    whole = lax.all_gather(snapshots, "row", axis=0, tiled=True)
    snap_count = whole.shape[0]
    feat_width = whole.shape[1]
    col_block = snap_count // col_count
    row_block = snapshots.shape[0]
    squares = jnp.sum(jnp.square(whole.astype(jnp.float32)), axis=1)
    padded_rows = jnp.concatenate([jnp.zeros((lag_count, feat_width), whole.dtype), whole], 0)
    padded_norms = jnp.concatenate([jnp.zeros((lag_count,), jnp.float32), squares], 0)
    row_start = row_at * row_block
    ext_rows = lax.dynamic_slice_in_dim(padded_rows, row_start, row_block + lag_count, 0)
    ext_norms = lax.dynamic_slice_in_dim(padded_norms, row_start, row_block + lag_count, 0)
    row_times = row_start - lag_count + jnp.arange(row_block + lag_count, dtype=jnp.int32)
    span = col_block + lag_count
    blocks = whole.reshape(col_count, col_block, feat_width)
    earlier = jnp.concatenate(
        [jnp.zeros((1, lag_count, feat_width), whole.dtype), blocks[:-1, col_block - lag_count :]],
        0,
    )
    source_rows = jnp.concatenate([earlier, blocks], 1).reshape(col_count * span, feat_width)
    norm_blocks = squares.reshape(col_count, col_block)
    norm_earlier = jnp.concatenate(
        [jnp.zeros((1, lag_count), jnp.float32), norm_blocks[:-1, col_block - lag_count :]], 0
    )
    source_norms = jnp.concatenate([norm_earlier, norm_blocks], 1).reshape(col_count * span)
    virtual = jnp.arange(span * lax.axis_size("col"), dtype=jnp.int32)
    times = virtual // span * col_block + virtual % span - lag_count
    inner = lax.dot_general(
        source_rows, ext_rows, (((1,), (1,)), ((), ())), preferred_element_type=jnp.float32
    )
    term = source_norms[:, None] + ext_norms[None, :] - 2.0 * inner
    keep = (times >= 0)[:, None] & (row_times >= 0)[None, :]
    tile = lax.psum_scatter(
        jnp.where(keep, term, 0.0).astype(jnp.bfloat16), "col", scatter_dimension=0, tiled=True
    ).astype(jnp.float32)
    window = 1
    while window < lag_count:
        tile = tile[window:, window:] + tile[:-window, :-window]
        window = window * 2
    lagged = tile[1:, 1:]
    step_rows = math.gcd(row_block, 16)
    block_count = row_block // step_rows
    slot_count = neighbours.shape[1]
    offset = neighbours - col_at * col_block
    inside = (offset >= 0) & (offset < col_block)
    tile_positions = jnp.arange(col_block, dtype=jnp.int32)

    def pick_block(pair):
        offs, lag_rows = pair
        match = offs[:, :, None] == tile_positions[None, None, :]
        return jnp.sum(jnp.where(match, lag_rows[:, None, :], 0.0), axis=2)

    chosen = lax.map(
        pick_block,
        (
            offset.reshape(block_count, step_rows, slot_count),
            lagged.T.reshape(block_count, step_rows, col_block),
        ),
    )
    chosen = chosen.reshape(row_block, slot_count)
    kernel_part = jnp.where(inside, 1.0 / (1.0 + chosen / (LAGS * FEATURES)), 0.0)
    slot_kernel = lax.psum(kernel_part, "col")
    mass = jnp.sum(slot_kernel, axis=1)
    markov = slot_kernel / mass[:, None]
    snap_positions = jnp.arange(snap_count, dtype=jnp.int32)

    def operator_block(pair):
        ids, weights = pair
        match = ids[:, :, None] == snap_positions[None, None, :]
        return jnp.sum(jnp.where(match, weights[:, :, None], 0.0), axis=1)

    transition = lax.map(
        operator_block,
        (
            neighbours.reshape(block_count, step_rows, slot_count),
            markov.reshape(block_count, step_rows, slot_count),
        ),
    )
    transition = transition.reshape(row_block, snap_count)
    piece_width = snap_count // (row_count * col_count)

    def apply_rows(basis_rows):
        return lax.dot_general(
            basis_rows,
            transition,
            (((1,), (1,)), ((), ())),
            precision=lax.Precision.HIGHEST,
            preferred_element_type=jnp.float32,
        )

    def own_piece(image):
        return lax.dynamic_slice_in_dim(image, col_at * piece_width, piece_width, 1)

    basis = start_basis
    for step in range(ITERS):
        piece = own_piece(apply_rows(basis))
        partial_gram = jnp.dot(
            piece, piece.T, precision=lax.Precision.HIGHEST, preferred_element_type=jnp.float32
        )
        gram_small = global_sum(partial_gram) / snap_count
        lower = jnp.linalg.cholesky(gram_small)
        basis = collect(jax.scipy.linalg.solve_triangular(lower, piece, lower=True))
    image_piece = own_piece(apply_rows(basis))
    basis_piece = lax.dynamic_slice_in_dim(
        basis, (row_at * col_count + col_at) * piece_width, piece_width, 1
    )
    partial_ray = jnp.dot(
        basis_piece,
        image_piece.T,
        precision=lax.Precision.HIGHEST,
        preferred_element_type=jnp.float32,
    )
    rayleigh = global_sum(partial_ray) / snap_count
    basis_rows = lax.dynamic_slice_in_dim(basis, row_start, row_block, 1)
    return (basis_rows, rayleigh)


def solution(mesh):
    placed = (P("row", "col"), P("row", None), P())
    return jax.shard_map(
        shards, mesh=mesh, in_specs=placed, out_specs=(P(None, "row"), P()), check_vma=False
    )
```

profile of v0, /device:TPU:1, one launch (start us, length us, event | category | flops | bytes accessed | tf_op | source)
XLA Modules:
  0.0 1007.9 jit_solution(16402256858035387622)
XLA Ops:
  8.0 90.6 %all-gather.2.cloned.1.call-done = bf16[4096,2048]{1,0:T(8,128)(2,1)} async-done(((bf16[512,2048]{1,0:T(8,128)(2,1)}), bf16[4096,2048]{1,0:T(8,128)(2,1)}) %all-gather.2.cloned.1.call-update) | async-done | bytes 16777232 | tf_op jit(solution)/shard_map/all_gather | solution.py:26
  98.6 7.2 multiply_reduce_fusion
  108.7 21.4 %fusion.5 = bf16[16,320,2048]{2,1,0:T(8,128)(2,1)} fusion(bf16[15,64,2048]{2,1,0:T(8,128)(2,1)S(1)} %slice.69, bf16[16,256,2048]{2,1,0:T(8,128)(2,1)} %bitcast.64), kind=kLoop, calls=%fused_computation.15 | loop fusion | flops 62914560 | bytes 41680896 | tf_op jit(solution)/shard_map/concatenate | solution.py:44
  130.2 23.8 %select_convert_fusion = bf16[5120,576]{1,0:T(8,128)(2,1)} fusion(bf16[5120,2048]{1,0:T(8,128)(2,1)} %bitcast.70, f32[576]{0:T(1024)S(1)} %pad_dynamic-slice_fusion.2, f32[5120]{0:T(1024)S(1)} %add.130, pred[576]{0:T(1024)(128)(4,1)S(1)} %add_compare_fusion, pred[5120]{0:T(1024)(128)(4,1)S(1)} %fusion.17, s32[]{:T(128)S(6)} %select_n.56, ...), kind=kOutput, calls=%fused_computation.17 | convolution fusion | flops 12097290240 | bytes 43675460 | tf_op jit(solution)/shard_map/dot_general | solution.py:52
  154.1 80.7 %reduce-scatter.2.cloned.1.call-done = bf16[320,576]{1,0:T(8,128)(2,1)} async-done(((bf16[5120,576]{1,0:T(8,128)(2,1)}), bf16[320,576]{1,0:T(8,128)(2,1)}) %reduce-scatter.2.cloned.1.call-update) | async-done | bytes 368656 | tf_op jit(solution)/shard_map/reduce_scatter | solution.py:57
  238.1 28.1 %while.22 = (s32[]{:T(128)}, f32[32,16,128]{2,1,0:T(8,128)S(1)}, s32[32,16,128]{2,1,0:T(8,128)S(1)}, f32[32,16,256]{2,1,0:T(8,128)S(1)}, s32[]{:T(128)}) while((s32[]{:T(128)}, f32[32,16,128]{2,1,0:T(8,128)S(1)}, s32[32,16,128]{2,1,0:T(8,128)S(1)}, f32[32,16,256]{2,1,0:T(8,128)S(1)}, s32[]{:T(128)}) %tuple.63), condition=%wide.region_4.5_spmd.clone, body=%wide.region_2.4_spmd.clone.sunk | while | flops 1570818 | bytes 98377 | solution.py:77
  267.0 83.3 %all-reduce.6.cloned.1.call-done = f32[512,128]{1,0:T(8,128)} async-done(((f32[512,128]{1,0:T(8,128)}), f32[512,128]{1,0:T(8,128)}) %all-reduce.6.cloned.1.call-update) | async-done | bytes 262160 | tf_op jit(solution)/shard_map/psum | solution.py:86
  352.5 280.2 %while.23 = (s32[]{:T(128)}, f32[32,16,4096]{2,1,0:T(8,128)}, s32[32,16,128]{2,1,0:T(8,128)S(1)}, f32[32,16,128]{2,1,0:T(8,128)S(1)}, s32[]{:T(128)}) while((s32[]{:T(128)}, f32[32,16,4096]{2,1,0:T(8,128)}, s32[32,16,128]{2,1,0:T(8,128)S(1)}, f32[32,16,128]{2,1,0:T(8,128)S(1)}, s32[]{:T(128)}) %tuple.64), condition=%wide.region_9.10_spmd.clone, body=%wide.region_7.9_spmd.clone.sunk | while | flops 25100288 | bytes 836165 | solution.py:96
  352.6 8.0 select_reduce_fusion.6
  361.3 8.0 select_reduce_fusion.6
  370.0 8.0 select_reduce_fusion.6
  378.8 8.0 select_reduce_fusion.6
  387.5 8.0 select_reduce_fusion.6
  396.3 8.0 select_reduce_fusion.6
  405.1 8.0 select_reduce_fusion.6
  413.8 8.0 select_reduce_fusion.6
  422.6 8.0 select_reduce_fusion.6
  431.4 8.0 select_reduce_fusion.6
  440.1 8.0 select_reduce_fusion.6
  448.9 8.0 select_reduce_fusion.6
  457.6 8.0 select_reduce_fusion.6
  466.4 8.0 select_reduce_fusion.6
  475.1 8.0 select_reduce_fusion.6
  483.9 8.0 select_reduce_fusion.6
  492.6 8.0 select_reduce_fusion.6
  501.4 8.0 select_reduce_fusion.6
  510.1 8.0 select_reduce_fusion.6
  518.9 8.0 select_reduce_fusion.6
  527.7 8.0 select_reduce_fusion.6
  536.4 8.0 select_reduce_fusion.6
  545.2 8.0 select_reduce_fusion.6
  553.9 8.0 select_reduce_fusion.6
  562.7 8.0 select_reduce_fusion.6
  571.4 8.0 select_reduce_fusion.6
  580.2 8.0 select_reduce_fusion.6
  589.0 8.0 select_reduce_fusion.6
  597.7 8.0 select_reduce_fusion.6
  606.5 8.0 select_reduce_fusion.6
  615.2 8.0 select_reduce_fusion.6
  623.9 8.0 select_reduce_fusion.6
  632.7 9.2 fusion.46
  642.1 65.8 %psum.29 = f32[32,32]{0,1:T(8,128)S(1)} all-reduce(f32[32,32]{0,1:T(8,128)S(1)} %fusion.36), channel_id=1, replica_groups=mesh['row'=8,'col'=16] {'row','col'}, use_global_device_ids=true, to_apply=%region_10.11 | all-reduce | flops 1024 | bytes 8192 | tf_op jit(solution)/shard_map/psum | solution.py:13
  714.8 63.7 %all_gather.10 = f32[32,4096]{0,1:T(8,128)S(1)} all-gather(f32[32,32]{0,1:T(8,128)S(1)} %fusion.23), channel_id=1, replica_groups=mesh['row'=8,'col'=16] {'row','col'}, dimensions={1}, use_global_device_ids=true | all-gather | bytes 528384 | tf_op jit(solution)/shard_map/all_gather | solution.py:17
  778.6 9.3 fusion.47
  788.1 65.0 %psum.30 = f32[32,32]{0,1:T(8,128)S(1)} all-reduce(f32[32,32]{0,1:T(8,128)S(1)} %fusion.33), channel_id=1, replica_groups=mesh['row'=8,'col'=16] {'row','col'}, use_global_device_ids=true, to_apply=%region_13.16 | all-reduce | flops 1024 | bytes 8192 | tf_op jit(solution)/shard_map/psum | solution.py:13
  860.2 65.1 %all_gather.11 = f32[32,4096]{0,1:T(8,128)S(1)} all-gather(f32[32,32]{0,1:T(8,128)S(1)} %fusion.20), channel_id=1, replica_groups=mesh['row'=8,'col'=16] {'row','col'}, dimensions={1}, use_global_device_ids=true | all-gather | bytes 528384 | tf_op jit(solution)/shard_map/all_gather | solution.py:17
  925.3 9.2 fusion.48
  934.8 65.0 %psum.31 = f32[32,32]{0,1:T(8,128)S(1)} all-reduce(f32[32,32]{0,1:T(8,128)S(1)} %fusion.29), channel_id=1, replica_groups=mesh['row'=8,'col'=16] {'row','col'}, use_global_device_ids=true, to_apply=%region_14.17 | all-reduce | flops 1024 | bytes 8192 | tf_op jit(solution)/shard_map/psum | solution.py:13
  (292 shorter events, 75.8 us)
Async XLA Ops:
  7.2 625.5 %copy-start = (f32[32,4096]{1,0:T(8,128)S(1)}, f32[32,4096]{1,0:T(8,128)}, u32[]{:S(2)}) copy-start(f32[32,4096]{1,0:T(8,128)} %param.12) | copy-start | bytes 1572868
  7.2 91.4 %all-gather.2.cloned.1.call-start = ((), (), s32[]{:S(2)}) async-start(), calls=%async_computation.1 | async-start | bytes 18874368 | tf_op jit(solution)/shard_map/all_gather | solution.py:26
  7.9 226.8 %reduce-scatter.2.cloned.1.call-start = ((), (), s32[]{:S(2)}) async-start(), calls=%async_computation.2 | async-start | bytes 6963200 | tf_op jit(solution)/shard_map/reduce_scatter | solution.py:57
  106.1 24.0 %slice-start = ((s8[16777216]{0:T(1024)(128)(4,1)}), s8[4194304]{0:T(1024)(128)(4,1)S(1)}, s32[]{:S(2)}) async-start(s8[16777216]{0:T(1024)(128)(4,1)} %bitcast.65), calls=%async_computation.4 | async-start | bytes 8388608
  108.7 21.5 %slice-start.1 = ((s8[16777216]{0:T(1024)(128)(4,1)}), s8[4194304]{0:T(1024)(128)(4,1)S(1)}, s32[]{:S(2)}) async-start(s8[16777216]{0:T(1024)(128)(4,1)} %bitcast.65), calls=%async_computation.5 | async-start | bytes 8388608
  108.7 21.4 %slice-start.2 = ((s8[16777216]{0:T(1024)(128)(4,1)}), s8[4194304]{0:T(1024)(128)(4,1)S(1)}, s32[]{:S(2)}) async-start(s8[16777216]{0:T(1024)(128)(4,1)} %bitcast.65), calls=%async_computation.6 | async-start | bytes 8388608
  108.7 21.4 %slice-start.3 = ((s8[16777216]{0:T(1024)(128)(4,1)}), s8[4194304]{0:T(1024)(128)(4,1)S(1)}, s32[]{:S(2)}) async-start(s8[16777216]{0:T(1024)(128)(4,1)} %bitcast.65), calls=%async_computation.7 | async-start | bytes 8388608
  130.1 23.9 %copy-start.1 = (s32[512,128]{1,0:T(8,128)S(1)}, s32[512,128]{1,0:T(8,128)}, u32[]{:S(2)}) copy-start(s32[512,128]{1,0:T(8,128)} %param.11) | copy-start | bytes 786436
  154.0 196.3 %all-reduce.6.cloned.1.call-start = ((), (), s32[]{:S(2)}) async-start(), calls=%async_computation.3 | async-start | bytes 524288 | tf_op jit(solution)/shard_map/psum | solution.py:86
Sparse Core Ops, SparseCore 0:
  9.7 88.8 all-gather.1
  154.1 80.6 reduce-scatter.1
  267.1 83.1 all-reduce.5
where the time goes:
time: 1020 us; the launch traced here: 1010 us
  other arithmetic  330 us (32%)
  blocking collectives  325 us (32%)
  waiting for transfers between devices  255 us (25%)
  matrix products  52.6 us (5%)
  local copies, waits for them, and re-layouts  29.2 us (3%)
  between operations  14.3 us (1%)
    reduce_sum x32, other arithmetic, operator_block(): return jnp.sum(jnp.where(match, weights[:, :, None], 0.0), axis=1)  256 us
    psum x3, blocking collectives, global_sum(): return lax.psum(value, ('row', 'col'))  196 us
    all_gather x2, blocking collectives, collect(): return lax.all_gather(columns, ('row', 'col'), axis=1, tiled=True)  129 us
    all_gather x1, waiting for transfers between devices, shards(): whole = lax.all_gather(snapshots, 'row', axis=0, tiled=True)  90.6 us
    psum x1, waiting for transfers between devices, shards(): slot_kernel = lax.psum(kernel_part, 'col')  83.3 us
    reduce_scatter x1, waiting for transfers between devices, shards(): lax.psum_scatter(jnp.where(keep, term, 0.0).astype(jnp.bfloat16), 'col',...  80.7 us
    dot_general x3, matrix products, apply_rows(): lax.dot_general(basis_rows, transition, (((1,), (1,)), ((), ())), precisi...  27.6 us
    reduce_sum x32, other arithmetic, pick_block(): return jnp.sum(jnp.where(match, lag_rows[:, None, :], 0.0), axis=2)  25.3 us
  transfers between devices with their start and end apart: 3, of which 3 were waited for; matrix products, arithmetic and copies ran while one was open for 0% of the time, Pallas kernels for 0%

commit v1 on v0

--- a/solution.py
+++ b/solution.py
@@ -9,8 +9,14 @@
 ITERS = 2
 
 
+def plan_ratios(view, net_axis, chip_axis):
+    for tick in (net_axis, chip_axis):
+        view = lax.psum(view, axis_name=tick)
+    return view
+
+
 def global_sum(value):
-    return lax.psum(value, ("row", "col"))
+    return plan_ratios(value, "row", "col")
 
 
 def collect(columns):

time: 1020 us -> 1100 us (1.078)
  blocking collectives: 325 us -> 405 us
    psum x3 -> x6, blocking collectives: 196 us -> 245 us  [plan_ratios(): view = lax.psum(view, axis_name=tick)]
    all_gather x2, blocking collectives: 129 us -> 160 us  [collect(): return lax.all_gather(columns, ('row', 'col'), axis=1, tiled=True)]
where the time goes in v1:
time: 1100 us; the launch traced here: 1090 us
  blocking collectives  405 us (37%)
  other arithmetic  330 us (30%)
  waiting for transfers between devices  255 us (23%)
  matrix products  52.7 us (5%)
  local copies, waits for them, and re-layouts  29.2 us (3%)
  between operations  14.1 us (1%)
    reduce_sum x32, other arithmetic, operator_block(): return jnp.sum(jnp.where(match, weights[:, :, None], 0.0), axis=1)  256 us
    psum x6, blocking collectives, plan_ratios(): view = lax.psum(view, axis_name=tick)  245 us
    all_gather x2, blocking collectives, collect(): return lax.all_gather(columns, ('row', 'col'), axis=1, tiled=True)  160 us
    all_gather x1, waiting for transfers between devices, shards(): whole = lax.all_gather(snapshots, 'row', axis=0, tiled=True)  90.6 us
    psum x1, waiting for transfers between devices, shards(): slot_kernel = lax.psum(kernel_part, 'col')  83.3 us
    reduce_scatter x1, waiting for transfers between devices, shards(): lax.psum_scatter(jnp.where(keep, term, 0.0).astype(jnp.bfloat16), 'col',...  80.7 us
    dot_general x3, matrix products, apply_rows(): lax.dot_general(basis_rows, transition, (((1,), (1,)), ((), ())), precisi...  27.7 us
    reduce_sum x32, other arithmetic, pick_block(): return jnp.sum(jnp.where(match, lag_rows[:, None, :], 0.0), axis=2)  25.3 us
  transfers between devices with their start and end apart: 3, of which 3 were waited for; matrix products, arithmetic and copies ran while one was open for 0% of the time, Pallas kernels for 0%

profile of v1, /device:TPU:1, one launch (start us, length us, event | category | flops | bytes accessed | tf_op | source)
XLA Modules:
  0.0 1087.8 jit_solution(3759189856232977223)
XLA Ops:
  8.0 90.6 %all-gather.2.cloned.1.call-done = bf16[4096,2048]{1,0:T(8,128)(2,1)} async-done(((bf16[512,2048]{1,0:T(8,128)(2,1)}), bf16[4096,2048]{1,0:T(8,128)(2,1)}) %all-gather.2.cloned.1.call-update) | async-done | bytes 16777232 | tf_op jit(solution)/shard_map/all_gather | solution.py:32
  108.7 21.4 %fusion.5 = bf16[16,320,2048]{2,1,0:T(8,128)(2,1)} fusion(bf16[15,64,2048]{2,1,0:T(8,128)(2,1)S(1)} %slice.69, bf16[16,256,2048]{2,1,0:T(8,128)(2,1)} %bitcast.64), kind=kLoop, calls=%fused_computation.15 | loop fusion | flops 62914560 | bytes 41680896 | tf_op jit(solution)/shard_map/concatenate | solution.py:50
  130.2 23.8 %select_convert_fusion = bf16[5120,576]{1,0:T(8,128)(2,1)} fusion(bf16[5120,2048]{1,0:T(8,128)(2,1)} %bitcast.70, f32[576]{0:T(1024)S(1)} %pad_dynamic-slice_fusion.2, f32[5120]{0:T(1024)S(1)} %add.136, pred[576]{0:T(1024)(128)(4,1)S(1)} %add_compare_fusion, pred[5120]{0:T(1024)(128)(4,1)S(1)} %fusion.17, s32[]{:T(128)S(6)} %select_n.56, ...), kind=kOutput, calls=%fused_computation.17 | convolution fusion | flops 12097290240 | bytes 43675460 | tf_op jit(solution)/shard_map/dot_general | solution.py:58
  154.1 80.7 %reduce-scatter.2.cloned.1.call-done = bf16[320,576]{1,0:T(8,128)(2,1)} async-done(((bf16[5120,576]{1,0:T(8,128)(2,1)}), bf16[320,576]{1,0:T(8,128)(2,1)}) %reduce-scatter.2.cloned.1.call-update) | async-done | bytes 368656 | tf_op jit(solution)/shard_map/reduce_scatter | solution.py:63
  238.2 27.8 %while.22 = (s32[]{:T(128)}, f32[32,16,128]{2,1,0:T(8,128)S(1)}, s32[32,16,128]{2,1,0:T(8,128)S(1)}, f32[32,16,256]{2,1,0:T(8,128)S(1)}, s32[]{:T(128)}) while((s32[]{:T(128)}, f32[32,16,128]{2,1,0:T(8,128)S(1)}, s32[32,16,128]{2,1,0:T(8,128)S(1)}, f32[32,16,256]{2,1,0:T(8,128)S(1)}, s32[]{:T(128)}) %tuple.63), condition=%wide.region_4.5_spmd.clone, body=%wide.region_2.4_spmd.clone.sunk | while | flops 1570818 | bytes 98377 | solution.py:83
  266.8 83.3 %all-reduce.6.cloned.1.call-done = f32[512,128]{1,0:T(8,128)} async-done(((f32[512,128]{1,0:T(8,128)}), f32[512,128]{1,0:T(8,128)}) %all-reduce.6.cloned.1.call-update) | async-done | bytes 262160 | tf_op jit(solution)/shard_map/psum | solution.py:92
  352.3 280.2 %while.23 = (s32[]{:T(128)}, f32[32,16,4096]{2,1,0:T(8,128)}, s32[32,16,128]{2,1,0:T(8,128)S(1)}, f32[32,16,128]{2,1,0:T(8,128)S(1)}, s32[]{:T(128)}) while((s32[]{:T(128)}, f32[32,16,4096]{2,1,0:T(8,128)}, s32[32,16,128]{2,1,0:T(8,128)S(1)}, f32[32,16,128]{2,1,0:T(8,128)S(1)}, s32[]{:T(128)}) %tuple.64), condition=%wide.region_9.10_spmd.clone, body=%wide.region_7.9_spmd.clone.sunk | while | flops 25100288 | bytes 836165 | solution.py:102
  361.1 8.0 select_reduce_fusion.6
  369.9 8.0 select_reduce_fusion.6
  378.6 8.0 select_reduce_fusion.6
  387.4 8.0 select_reduce_fusion.6
  396.1 8.0 select_reduce_fusion.6
  404.9 8.0 select_reduce_fusion.6
  413.6 8.0 select_reduce_fusion.6
  422.4 8.0 select_reduce_fusion.6
  431.2 8.0 select_reduce_fusion.6
  439.9 8.0 select_reduce_fusion.6
  448.7 8.0 select_reduce_fusion.6
  457.4 8.0 select_reduce_fusion.6
  466.2 8.0 select_reduce_fusion.6
  475.0 8.0 select_reduce_fusion.6
  483.7 8.0 select_reduce_fusion.6
  492.5 8.0 select_reduce_fusion.6
  509.9 8.0 select_reduce_fusion.6
  518.7 8.0 select_reduce_fusion.6
  527.5 8.0 select_reduce_fusion.6
  536.2 8.0 select_reduce_fusion.6
  545.0 8.0 select_reduce_fusion.6
  553.8 8.0 select_reduce_fusion.6
  562.5 8.0 select_reduce_fusion.6
  571.3 8.0 select_reduce_fusion.6
  580.0 8.0 select_reduce_fusion.6
  588.8 8.0 select_reduce_fusion.6
  597.5 8.0 select_reduce_fusion.6
  606.3 8.0 select_reduce_fusion.6
  615.0 8.0 select_reduce_fusion.6
  623.8 8.0 select_reduce_fusion.6
  632.5 9.2 fusion.46
  642.0 22.9 %psum.50 = f32[32,32]{0,1:T(8,128)S(1)} all-reduce(f32[32,32]{0,1:T(8,128)S(1)} %fusion.36), channel_id=1, replica_groups=mesh['row'=8,'col'=16] {'row'}, use_global_device_ids=true, to_apply=%region_10.11 | all-reduce | flops 1024 | bytes 8192 | tf_op jit(solution)/shard_map/psum | solution.py:14
  664.9 58.1 %psum.51 = f32[32,32]{0,1:T(8,128)S(1)} all-reduce(f32[32,32]{0,1:T(8,128)S(1)} %psum.50), channel_id=1, replica_groups=mesh['row'=8,'col'=16] {'col'}, use_global_device_ids=true, to_apply=%region_11.12 | all-reduce | flops 1024 | bytes 8192 | tf_op jit(solution)/shard_map/psum | solution.py:14
  730.0 80.1 %all_gather.10 = f32[32,4096]{0,1:T(8,128)S(1)} all-gather(f32[32,32]{0,1:T(8,128)S(1)} %fusion.23), channel_id=1, replica_groups=mesh['row'=8,'col'=16] {'row','col'}, dimensions={1}, use_global_device_ids=true | all-gather | bytes 528384 | tf_op jit(solution)/shard_map/all_gather | solution.py:23
  810.1 9.3 fusion.47
  819.6 23.6 %psum.52 = f32[32,32]{0,1:T(8,128)S(1)} all-reduce(f32[32,32]{0,1:T(8,128)S(1)} %fusion.33), channel_id=1, replica_groups=mesh['row'=8,'col'=16] {'row'}, use_global_device_ids=true, to_apply=%region_14.17 | all-reduce | flops 1024 | bytes 8192 | tf_op jit(solution)/shard_map/psum | solution.py:14
  843.2 58.2 %psum.53 = f32[32,32]{0,1:T(8,128)S(1)} all-reduce(f32[32,32]{0,1:T(8,128)S(1)} %psum.52), channel_id=1, replica_groups=mesh['row'=8,'col'=16] {'col'}, use_global_device_ids=true, to_apply=%region_15.18 | all-reduce | flops 1024 | bytes 8192 | tf_op jit(solution)/shard_map/psum | solution.py:14
  908.5 80.1 %all_gather.11 = f32[32,4096]{0,1:T(8,128)S(1)} all-gather(f32[32,32]{0,1:T(8,128)S(1)} %fusion.20), channel_id=1, replica_groups=mesh['row'=8,'col'=16] {'row','col'}, dimensions={1}, use_global_device_ids=true | all-gather | bytes 528384 | tf_op jit(solution)/shard_map/all_gather | solution.py:23
  988.6 9.3 fusion.48
  998.1 23.6 %psum.54 = f32[32,32]{0,1:T(8,128)S(1)} all-reduce(f32[32,32]{0,1:T(8,128)S(1)} %fusion.29), channel_id=1, replica_groups=mesh['row'=8,'col'=16] {'row'}, use_global_device_ids=true, to_apply=%region_16.19 | all-reduce | flops 1024 | bytes 8192 | tf_op jit(solution)/shard_map/psum | solution.py:14
  1021.6 58.2 %psum.55 = f32[32,32]{0,1:T(8,128)S(1)} all-reduce(f32[32,32]{0,1:T(8,128)S(1)} %psum.54), channel_id=1, replica_groups=mesh['row'=8,'col'=16] {'col'}, use_global_device_ids=true, to_apply=%region_17.20 | all-reduce | flops 1024 | bytes 8192 | tf_op jit(solution)/shard_map/psum | solution.py:14
  (295 shorter events, 99.0 us)
Async XLA Ops:
  7.2 625.4 %copy-start = (f32[32,4096]{1,0:T(8,128)S(1)}, f32[32,4096]{1,0:T(8,128)}, u32[]{:S(2)}) copy-start(f32[32,4096]{1,0:T(8,128)} %param.12) | copy-start | bytes 1572868
  7.2 91.4 %all-gather.2.cloned.1.call-start = ((), (), s32[]{:S(2)}) async-start(), calls=%async_computation.1 | async-start | bytes 18874368 | tf_op jit(solution)/shard_map/all_gather | solution.py:32
  7.9 226.9 %reduce-scatter.2.cloned.1.call-start = ((), (), s32[]{:S(2)}) async-start(), calls=%async_computation.2 | async-start | bytes 6963200 | tf_op jit(solution)/shard_map/reduce_scatter | solution.py:63
  106.1 24.0 %slice-start = ((s8[16777216]{0:T(1024)(128)(4,1)}), s8[4194304]{0:T(1024)(128)(4,1)S(1)}, s32[]{:S(2)}) async-start(s8[16777216]{0:T(1024)(128)(4,1)} %bitcast.65), calls=%async_computation.4 | async-start | bytes 8388608
  108.7 21.5 %slice-start.1 = ((s8[16777216]{0:T(1024)(128)(4,1)}), s8[4194304]{0:T(1024)(128)(4,1)S(1)}, s32[]{:S(2)}) async-start(s8[16777216]{0:T(1024)(128)(4,1)} %bitcast.65), calls=%async_computation.5 | async-start | bytes 8388608
  108.7 21.4 %slice-start.2 = ((s8[16777216]{0:T(1024)(128)(4,1)}), s8[4194304]{0:T(1024)(128)(4,1)S(1)}, s32[]{:S(2)}) async-start(s8[16777216]{0:T(1024)(128)(4,1)} %bitcast.65), calls=%async_computation.6 | async-start | bytes 8388608
  108.7 21.4 %slice-start.3 = ((s8[16777216]{0:T(1024)(128)(4,1)}), s8[4194304]{0:T(1024)(128)(4,1)S(1)}, s32[]{:S(2)}) async-start(s8[16777216]{0:T(1024)(128)(4,1)} %bitcast.65), calls=%async_computation.7 | async-start | bytes 8388608
  130.1 23.9 %copy-start.1 = (s32[512,128]{1,0:T(8,128)S(1)}, s32[512,128]{1,0:T(8,128)}, u32[]{:S(2)}) copy-start(s32[512,128]{1,0:T(8,128)} %param.11) | copy-start | bytes 786436
  154.0 196.2 %all-reduce.6.cloned.1.call-start = ((), (), s32[]{:S(2)}) async-start(), calls=%async_computation.3 | async-start | bytes 524288 | tf_op jit(solution)/shard_map/psum | solution.py:92
Sparse Core Ops, SparseCore 0:
  9.7 88.8 all-gather.1
  154.1 80.6 reduce-scatter.1
  266.9 83.1 all-reduce.5
